TPU v7x, 32 devices: a whole 2x2x4 slice. The times are simulated.
32 devices in a mesh: groups: 2 (over x), worker: 2 (over core), tensor: 8 (over z, y).
Axes of the slice: x: 2, y: 2, z: 4, core: 2. Of those that a mesh axis runs over, the one named last changes fastest.
Arguments:
- tokens: bfloat16 [1024, 8192], P(('groups', 'worker'), 'tensor'), parts along dimension 0, may hold values from -6 to 6
- norm_gain: float32 [8192], replicated, may hold values from 0.5 to 1.5
- query_weight: bfloat16 [8192, 8192], P(None, 'tensor'), may hold values from -0.0625 to 0.0625
- key_weight: bfloat16 [8192, 1024], P(None, 'tensor'), may hold values from -0.15625 to 0.15625
- value_weight: bfloat16 [8192, 1024], P(None, 'tensor'), may hold values from -0.0625 to 0.0625
- output_weight: bfloat16 [8192, 8192], P('tensor'), may hold values from -0.0625 to 0.0625
- cached_blocks: bfloat16 [8, 1024, 2, 1024], P(('groups', 'worker'), 'tensor'), parts along dimension 0
- cache_length: int32 [8], P('groups'), parts along dimension 0, may hold values from 256 to 1024, as said below
- block_table: int32 [8, 64], P('groups'), parts along dimension 0, may hold values from 0 to 63, each once within a row
- destination: int32 [8], P('groups'), parts along dimension 0, may hold values from 0 to 1, as said below
Outputs:
- attended: bfloat16 [4, 3, 128, 8192], P(('groups', 'worker'), None, None, 'tensor'), parts along dimension 0
There are 2 independent parts, one for each index of `groups`. A program takes and returns all parts, laid end to end along the dimension named above; an argument that names none is the same for every part. Nothing has to cross between parts.
Inputs may be any that keep to these rules, and one draw needn't show every extreme that they name: Exactly 3 sequences have one destination, the others the other; which one is drawn. `cache_length`: some sequence has exactly 1024 cached tokens.
All inputs are finite; a program needn't handle non-finite values.
Results may differ from a plain program's by a relative error of at most 0.02.
The roundings to bfloat16 on the way count: a program that leaves them out, or rounds other values in their place, can miss the bound.
Values may be sent and summed in bfloat16 or wider, within the bound.
No kernel may reach another device: no remote copies, remote signals or barrier semaphores. Data moves between devices by JAX's collectives and lax.ppermute only.
A program may use at most 128 MiB of HBM per device.

v0:
```python
import math
import jax
import jax.numpy as jnp
from jax import lax
from jax.sharding import PartitionSpec as P

D = 8192
KVH = 8
HD = 128
NEW = 128
BLK = 16
CAP = 3
epsilon = 1e-05


def from_partner(block, axis, bit):
    count = lax.axis_size(axis)
    route = []
    for low in range(count):
        high = low | 1 << bit
        if high != low and high < count:
            route += [(low, high), (high, low)]
    return lax.ppermute(block, axis, route)


def rotate(values, positions):
    halfway = HD // 2
    inverse = 500000.0 ** (-(jnp.arange(halfway, dtype=jnp.float32) * 2.0 / HD))
    angles = positions[:, None] * inverse[None, :]
    cosine_table = jnp.concatenate([jnp.cos(angles), jnp.cos(angles)], axis=-1)[:, None, :]
    sine_table = jnp.concatenate([jnp.sin(angles), jnp.sin(angles)], axis=-1)[:, None, :]
    turned = jnp.concatenate([-values[..., halfway:], values[..., :halfway]], axis=-1)
    return values * cosine_table + turned * sine_table


def attend(
    token_rows,
    blocks,
    lengths,
    tables,
    norm_gain,
    query_weight,
    key_weight,
    value_weight,
    output_weight,
):
    tensor_count = lax.axis_size("tensor")
    tensor_index = lax.axis_index("tensor")
    group_width = tensor_count // KVH
    bit_count = group_width.bit_length() - 1
    seq_count = blocks.shape[0]
    total = token_rows.shape[0]
    query_cols = query_weight.shape[1]
    widened = lax.all_gather(token_rows, "tensor", axis=1, tiled=True).astype(jnp.float32)
    scaled = (widened * norm_gain[None, :]).astype(jnp.bfloat16)
    query_sum = jnp.dot(scaled, query_weight, preferred_element_type=jnp.float32)
    key_sum = jnp.dot(scaled, key_weight, preferred_element_type=jnp.float32)
    value_sum = jnp.dot(scaled, value_weight, preferred_element_type=jnp.float32)
    squares = jnp.sum(widened * widened, axis=1)
    factor = lax.rsqrt(squares / D + epsilon)[:, None]
    positions = (
        (lengths[:, None] + jnp.arange(NEW, dtype=jnp.int32)[None, :])
        .reshape(total)
        .astype(jnp.float32)
    )
    heads_here = query_cols // HD
    queries = rotate((query_sum * factor).reshape(total, heads_here, HD), positions).astype(
        jnp.bfloat16
    )
    key_full = (key_sum * factor).astype(jnp.bfloat16)
    value_full = (value_sum * factor).astype(jnp.bfloat16)
    for bit in range(bit_count):
        other_key, other_value = from_partner((key_full, value_full), "tensor", bit)
        upper = tensor_index // (1 << bit) % 2 == 1
        key_full = jnp.where(
            upper,
            jnp.concatenate([other_key, key_full], axis=1),
            jnp.concatenate([key_full, other_key], axis=1),
        )
        value_full = jnp.where(
            upper,
            jnp.concatenate([other_value, value_full], axis=1),
            jnp.concatenate([value_full, other_value], axis=1),
        )
    new_key = rotate(key_full.astype(jnp.float32)[:, None, :], positions)[:, 0, :].astype(
        jnp.bfloat16
    )
    fresh_keys = new_key.reshape(seq_count, NEW, HD)
    fresh_values = value_full.reshape(seq_count, NEW, HD)
    local_tokens = blocks.shape[1]
    inverse_root = 1.0 / math.sqrt(HD)
    query_blocks = queries.reshape(seq_count, NEW, heads_here, HD)
    causal = jnp.arange(NEW)[:, None] >= jnp.arange(NEW)[None, :]
    spread = jnp.repeat(
        blocks.reshape(seq_count, local_tokens, 2, KVH, HD), tensor_count // KVH, axis=3
    )
    arrived = lax.all_to_all(spread, "tensor", split_axis=3, concat_axis=1, tiled=True)
    context = arrived.shape[1]
    old_key = arrived[:, :, 0, 0, :]
    old_value = arrived[:, :, 1, 0, :]
    stored = jnp.arange(context, dtype=jnp.int32)
    logical = jnp.take(tables, stored // BLK, axis=1) * BLK + stored % BLK
    visible = logical < lengths[:, None]
    old_scores = (
        jnp.einsum("sqhd,skd->shqk", query_blocks, old_key, preferred_element_type=jnp.float32)
        * inverse_root
    )
    old_scores = jnp.where(visible[:, None, None, :], old_scores, -1e30)
    new_scores = (
        jnp.einsum("sqhd,skd->shqk", query_blocks, fresh_keys, preferred_element_type=jnp.float32)
        * inverse_root
    )
    new_scores = jnp.where(causal[None, None], new_scores, -1e30)
    largest = jnp.maximum(jnp.max(old_scores, axis=3), jnp.max(new_scores, axis=3))[..., None]
    old_expo = jnp.exp(old_scores - largest)
    new_expo = jnp.exp(new_scores - largest)
    denominator = (jnp.sum(old_expo, axis=3) + jnp.sum(new_expo, axis=3))[..., None]
    old_probs = (old_expo / denominator).astype(jnp.bfloat16)
    new_probs = (new_expo / denominator).astype(jnp.bfloat16)
    mixture = jnp.einsum("shqk,skd->sqhd", old_probs, old_value, preferred_element_type=jnp.float32)
    mixture = mixture + jnp.einsum(
        "shqk,skd->sqhd", new_probs, fresh_values, preferred_element_type=jnp.float32
    )
    attended_rows = mixture.astype(jnp.bfloat16).reshape(total, heads_here * HD)
    partial_value = jnp.dot(attended_rows, output_weight, preferred_element_type=jnp.float32)
    summed = lax.psum_scatter(partial_value, "tensor", scatter_dimension=1, tiled=True)
    return summed.astype(jnp.bfloat16)


def local(
    tokens,
    norm_gain,
    query_weight,
    key_weight,
    value_weight,
    output_weight,
    cached_blocks,
    cache_length,
    block_table,
    destination,
):
    worker_index = lax.axis_index("worker")
    seq_total = destination.shape[0]
    belongs = (destination == worker_index).astype(jnp.int32)
    ranking = jnp.cumsum(belongs) - 1
    matched = (belongs[None, :] == 1) & (
        ranking[None, :] == jnp.arange(CAP, dtype=jnp.int32)[:, None]
    )
    slot_owner = jnp.sum(
        matched.astype(jnp.int32) * jnp.arange(seq_total, dtype=jnp.int32)[None, :], axis=1
    )
    occupied = jnp.any(matched, axis=1)
    local_count = cached_blocks.shape[0]
    owned = worker_index * local_count + jnp.arange(local_count, dtype=jnp.int32)
    mixed = attend(
        tokens,
        cached_blocks,
        jnp.take(cache_length, owned),
        jnp.take(block_table, owned, axis=0),
        norm_gain,
        query_weight,
        key_weight,
        value_weight,
        output_weight,
    )
    everyone = lax.all_gather(mixed, "worker", axis=0, tiled=True)
    placed = jnp.take(everyone.reshape(seq_total, NEW, -1), slot_owner, axis=0)
    result = jnp.where(occupied[:, None, None], placed, jnp.zeros_like(placed))
    return result[None]


def solution(mesh):
    placed = (
        P(("groups", "worker"), "tensor"),
        P(),
        P(None, "tensor"),
        P(None, "tensor"),
        P(None, "tensor"),
        P("tensor", None),
        P(("groups", "worker"), "tensor", None, None),
        P("groups"),
        P("groups", None),
        P("groups"),
    )
    return jax.shard_map(
        local,
        mesh=mesh,
        in_specs=placed,
        out_specs=P(("groups", "worker"), None, None, "tensor"),
        check_vma=False,
    )
```

profile of v0, /device:TPU:0, one launch (start us, length us, event | category | flops | bytes accessed | tf_op | source)
XLA Modules:
  0.0 310.5 jit_solution(4129475814052174620)
XLA Ops:
  6.5 0.0 copy-start
  6.5 0.0 all-gather.3.cloned.1.call-start
  6.5 0.7 all-gather.3.cloned.1.call-update
  7.3 2.6 copy.86
  9.8 1.3 copy.87
  11.1 7.3 %all-to-all-start = ((bf16[2,128,2,8,128]{4,1,0,2,3:T(8,128)(2,1)}), bf16[2,128,2,8,128]{4,1,0,2,3:T(8,128)(2,1)S(1)}, u32[]{:S(2)}, u32[]{:S(2)}) async-start(bf16[2,128,2,8,128]{4,1,0,2,3:T(8,128)(2,1)} %copy.87), calls=%async_computation | async-start | bytes 2097152 | tf_op jit(solution)/shard_map/all_to_all | solution.py:97
  18.4 0.0 reduce-scatter.2.cloned.1.call-start
  18.5 1.3 gather_fusion.2
  19.8 1.3 gather_fusion
  21.1 0.1 broadcast_select_fusion
  21.2 0.1 copy.80
  21.3 4.0 %gather_fusion.1 = s32[1024,2]{1,0:T(8,128)} fusion(s32[2,64]{0,1:T(8,128)S(1)} %copy.80, s32[1024]{0:T(1024)S(1)} %broadcast_clamp_fusion), kind=kCustom, calls=%fused_computation.1 | custom fusion | bytes 20480 | tf_op jit(solution)/shard_map/jit(_take)/gather | solution.py:102
  25.3 1.2 copy.81
  26.6 0.6 iota_compare_fusion
  27.2 0.1 fusion.68
  27.3 0.5 multiply_cosine_fusion
  27.8 0.1 pad_maximum_fusion
  28.0 0.1 compare_bitcast_fusion
  28.0 0.3 multiply_sine_fusion.1
  28.3 32.7 %all-to-all-done = bf16[2,128,2,8,128]{4,1,0,2,3:T(8,128)(2,1)S(1)} async-done(((bf16[2,128,2,8,128]{4,1,0,2,3:T(8,128)(2,1)}), bf16[2,128,2,8,128]{4,1,0,2,3:T(8,128)(2,1)S(1)}, u32[]{:S(2)}, u32[]{:S(2)}) %all-to-all-start) | async-done | bytes 1048608 | tf_op jit(solution)/shard_map/all_to_all | solution.py:97
  61.1 1.0 copy.88
  62.1 40.3 %all-gather.3.cloned.1.call-done = bf16[256,8192]{1,0:T(8,128)(2,1)} async-done(((bf16[256,1024]{1,0:T(8,128)(2,1)}), bf16[256,8192]{1,0:T(8,128)(2,1)}) %all-gather.3.cloned.1.call-update) | async-done | bytes 4194320 | tf_op jit(solution)/shard_map/all_gather | solution.py:54
  102.4 3.1 fusion.1
  105.5 0.0 copy-done
  105.5 3.6 %fusion.25 = bf16[256,128]{0,1:T(8,128)(2,1)S(1)} fusion(bf16[8192,128]{1,0:T(8,128)(2,1)S(1)} %copy-done, bf16[256,8192]{1,0:T(8,128)(2,1)} %all-gather.3.cloned.1.call-done, f32[8192]{0:T(1024)} %param.11, f32[256]{0:T(256)S(1)} %add_rsqrt_fusion), kind=kOutput, calls=%fused_computation.28 | convolution fusion | flops 543227904 | bytes 6390784 | tf_op jit(solution)/shard_map/dot_general | solution.py:58
  109.1 0.6 reshape.302
  109.7 0.0 copy-done.6
  109.7 4.3 %fusion.31 = f32[256,128]{0,1:T(8,128)S(1)} fusion(bf16[8192,128]{1,0:T(8,128)(2,1)} %param.13, bf16[256,8192]{1,0:T(8,128)(2,1)} %all-gather.3.cloned.1.call-done, f32[8192]{0:T(1024)S(1)} %copy-done.6, f32[256]{0:T(256)S(1)} %add_rsqrt_fusion), kind=kOutput, calls=%fused_computation.30 | convolution fusion | flops 543260672 | bytes 6456320 | tf_op jit(solution)/shard_map/dot_general | solution.py:57
  114.1 0.1 copy.106
  114.2 9.5 %fusion.11 = f32[256,1024]{1,0:T(8,128)S(1)} fusion(bf16[8192,1024]{1,0:T(8,128)(2,1)} %param.12, bf16[256,8192]{1,0:T(8,128)(2,1)} %all-gather.3.cloned.1.call-done, f32[8192]{0:T(1024)} %param.11, f32[256]{0:T(256)S(1)} %add_rsqrt_fusion), kind=kOutput, calls=%fused_computation.18 | convolution fusion | flops 4301520896 | bytes 22053888 | tf_op jit(solution)/shard_map/dot_general | solution.py:56
  123.8 0.3 copy.109
  124.1 0.2 copy.110
  124.3 0.9 slice_negate_fusion
  125.2 0.4 copy.104
  125.6 1.5 copy.105
  127.1 0.4 fusion.35
  127.5 0.3 fusion.69
  127.8 0.0 copy-start.2
  127.8 2.6 bitcast_reduce_fusion
  130.5 0.2 fusion.36
  130.6 0.0 slice-start
  130.6 2.1 fusion.3
  132.8 0.0 slice-start.1
  132.8 0.0 slice-start.2
  132.8 0.0 slice-start.3
  132.8 2.5 fusion.17
  135.3 0.4 fusion.18
  135.7 0.3 copy.96
  136.1 0.1 slice-done.2
  136.2 1.2 slice-done.3
  137.4 6.7 %fusion.38 = f32[256,8192]{1,0:T(8,128)} fusion(bf16[1024,8192]{1,0:T(8,128)(2,1)S(1)} %bitcast.101, bf16[32,8,8,128]{3,2,1,0:T(8,128)(2,1)S(1)} %bitcast.109), kind=kOutput, calls=%fused_computation.40 | convolution fusion | flops 4294967296 | bytes 25690112 | tf_op jit(solution)/shard_map/dot_general | solution.py:125
  144.1 0.0 reduce-scatter.2.cloned.1.call-update
  144.2 0.0 all-gather.5.cloned.1.call-start
  144.2 146.5 %reduce-scatter.2.cloned.1.call-done = f32[256,1024]{1,0:T(8,128)} async-done(((f32[256,8192]{1,0:T(8,128)}), f32[256,1024]{1,0:T(8,128)}) %reduce-scatter.2.cloned.1.call-update) | async-done | bytes 1048592 | tf_op jit(solution)/shard_map/reduce_scatter | solution.py:126
  290.7 2.1 convert_element_type.67
  292.8 0.0 all-gather.5.cloned.1.call-update
  292.8 0.0 copy-done.5
  292.8 0.2 reduce-window.8
  293.0 0.1 select_reduce_fusion
  293.2 0.1 fusion.61
  293.3 7.8 %all-gather.5.cloned.1.call-done = bf16[512,1024]{1,0:T(8,128)(2,1)} async-done(((bf16[256,1024]{1,0:T(8,128)(2,1)}), bf16[512,1024]{1,0:T(8,128)(2,1)}) %all-gather.5.cloned.1.call-update) | async-done | bytes 1048592 | tf_op jit(solution)/shard_map/all_gather | solution.py:166
  301.1 1.8 gather_fusion.3
  302.9 1.0 fusion.37
  304.0 0.0 copy-done.1
  (30 shorter events, 0.2 us)
Async XLA Ops:
  6.5 98.9 %copy-start = (bf16[8192,128]{1,0:T(8,128)(2,1)S(1)}, bf16[8192,128]{1,0:T(8,128)(2,1)}, u32[]{:S(2)}) copy-start(bf16[8192,128]{1,0:T(8,128)(2,1)} %param.14) | copy-start | bytes 6291460
  6.5 95.8 %all-gather.3.cloned.1.call-start = ((), (), s32[]{:S(2)}) async-start(), calls=%async_computation.2 | async-start | bytes 4718592 | tf_op jit(solution)/shard_map/all_gather | solution.py:54
  11.1 49.9 %all-to-all-start = ((bf16[2,128,2,8,128]{4,1,0,2,3:T(8,128)(2,1)}), bf16[2,128,2,8,128]{4,1,0,2,3:T(8,128)(2,1)S(1)}, u32[]{:S(2)}, u32[]{:S(2)}) async-start(bf16[2,128,2,8,128]{4,1,0,2,3:T(8,128)(2,1)} %copy.87), calls=%async_computation | async-start | bytes 2097152 | tf_op jit(solution)/shard_map/all_to_all | solution.py:97
  18.4 272.2 %reduce-scatter.2.cloned.1.call-start = ((), (), s32[]{:S(2)}) async-start(), calls=%async_computation.3 | async-start | bytes 9437184 | tf_op jit(solution)/shard_map/reduce_scatter | solution.py:126
  62.1 47.6 %copy-start.6 = (f32[8192]{0:T(1024)S(1)}, f32[8192]{0:T(1024)}, u32[]{:S(2)}) copy-start(f32[8192]{0:T(1024)} %param.11) | copy-start | bytes 98308
  123.8 3.7 %copy-start.3 = (pred[128,128]{0,1:T(8,128)(4,1)S(1)}, pred[128,128]{0,1:T(8,128)(4,1)}, u32[]{:S(2)}) copy-start(pred[128,128]{0,1:T(8,128)(4,1)} %iota_compare_fusion) | copy-start | bytes 49156
  127.8 4.9 %copy-start.2 = (bf16[2,8,128,2,1,128]{5,2,1,0,3,4:T(8,128)(2,1)S(1)}, bf16[2,8,128,2,1,128]{5,2,1,0,3,4:T(8,128)(2,1)}, u32[]{:S(2)}) copy-start(bf16[2,8,128,2,1,128]{5,2,1,0,3,4:T(8,128)(2,1)} %copy.88) | copy-start | bytes 3145732
  130.6 5.4 %slice-start = ((s8[16777216]{0:T(1024)(128)(4,1)}), s8[4194304]{0:T(1024)(128)(4,1)S(1)}, s32[]{:S(2)}) async-start(s8[16777216]{0:T(1024)(128)(4,1)} %bitcast.100), calls=%async_computation.5 | async-start | bytes 8388608
  132.8 2.5 copy-start.4
  132.8 3.3 %slice-start.1 = ((s8[16777216]{0:T(1024)(128)(4,1)}), s8[4194304]{0:T(1024)(128)(4,1)S(1)}, s32[]{:S(2)}) async-start(s8[16777216]{0:T(1024)(128)(4,1)} %bitcast.100), calls=%async_computation.6 | async-start | bytes 8388608
  132.8 3.4 %slice-start.2 = ((s8[16777216]{0:T(1024)(128)(4,1)}), s8[4194304]{0:T(1024)(128)(4,1)S(1)}, s32[]{:S(2)}) async-start(s8[16777216]{0:T(1024)(128)(4,1)} %bitcast.100), calls=%async_computation.7 | async-start | bytes 8388608
  132.8 4.6 %slice-start.3 = ((s8[16777216]{0:T(1024)(128)(4,1)}), s8[4194304]{0:T(1024)(128)(4,1)S(1)}, s32[]{:S(2)}) async-start(s8[16777216]{0:T(1024)(128)(4,1)} %bitcast.100), calls=%async_computation.8 | async-start | bytes 8388608
  137.4 166.6 %copy-start.1 = (bf16[8192,128]{1,0:T(8,128)(2,1)S(1)}, bf16[8192,128]{1,0:T(8,128)(2,1)}, u32[]{:S(2)}) copy-start(bf16[8192,128]{1,0:T(8,128)(2,1)} %param.14) | copy-start | bytes 6291460
  144.1 148.7 %copy-start.5 = (s32[4]{0:T(128)S(1)}, s32[4]{0:T(128)}, u32[]{:S(2)}) copy-start(s32[4]{0:T(128)} %param.19) | copy-start | bytes 52
  144.2 156.9 %all-gather.5.cloned.1.call-start = ((), (), s32[]{:S(2)}) async-start(), calls=%async_computation.4 | async-start | bytes 1572864 | tf_op jit(solution)/shard_map/all_gather | solution.py:166
Sparse Core Ops, SparseCore 0:
  9.5 92.8 all-gather.2
  144.3 146.3 reduce-scatter.1
  292.9 8.1 all-gather.4
where the time goes:
time: 311 us; the launch traced here: 310 us
  waiting for transfers between devices  228 us (73%)
  matrix products  30 us (10%)
  local copies, waits for them, and re-layouts  19.5 us (6%)
  between operations  13.5 us (4%)
  other arithmetic  12.2 us (4%)
  starting transfers between devices  7.39 us (2%)
    reduce_scatter x1, waiting for transfers between devices, attend(): lax.psum_scatter(partial_value, 'tensor', scatter_dimension=1, tiled=True)  146 us
    all_gather x1, waiting for transfers between devices, attend(): lax.all_gather(token_rows, 'tensor', axis=1, tiled=True).astype(jnp.float32)  40.3 us
    all_to_all x1, waiting for transfers between devices, attend(): lax.all_to_all(spread, 'tensor', split_axis=3, concat_axis=1, tiled=True)  32.7 us
    dot_general x1, matrix products, attend(): jnp.dot(scaled, query_weight, preferred_element_type=jnp.float32)  9.52 us
    all_gather x1, waiting for transfers between devices, local(): everyone = lax.all_gather(mixed, 'worker', axis=0, tiled=True)  7.81 us
    all_to_all x1, starting transfers between devices, attend(): lax.all_to_all(spread, 'tensor', split_axis=3, concat_axis=1, tiled=True)  7.31 us
    dot_general x1, matrix products, attend(): jnp.dot(attended_rows, output_weight, preferred_element_type=jnp.float32)  6.74 us
  transfers between devices with their start and end apart: 4, of which 4 were waited for; matrix products, arithmetic and copies ran while one was open for 5% of the time, Pallas kernels for 0%

commit v1 on v0

--- a/solution.py
+++ b/solution.py
@@ -51,7 +51,30 @@
     seq_count = blocks.shape[0]
     total = token_rows.shape[0]
     query_cols = query_weight.shape[1]
-    widened = lax.all_gather(token_rows, "tensor", axis=1, tiled=True).astype(jnp.float32)
+
+    def save_the_threads(payload):
+        store = []
+        item_now, seen_now, part_now = (
+            jax.lax.axis_size("tensor"),
+            jax.lax.axis_index("tensor"),
+            payload.shape[1],
+        )
+        for h, k0 in enumerate(payload.shape):
+            store.append(k0 * item_now if h == 1 else k0)
+        r_now = lax.dynamic_update_slice_in_dim(
+            jnp.zeros(store, payload.dtype), payload, seen_now * part_now, axis=1
+        )
+        for no in range(1, item_now):
+            kept_rows = []
+            for h in range(item_now):
+                kept_rows.append((h, (h + 1) % item_now))
+            payload = jax.lax.ppermute(payload, "tensor", kept_rows)
+            r_now = lax.dynamic_update_slice_in_dim(
+                r_now, payload, (seen_now - no) % item_now * part_now, axis=1
+            )
+        return r_now
+
+    widened = save_the_threads(token_rows).astype(jnp.float32)
     scaled = (widened * norm_gain[None, :]).astype(jnp.bfloat16)
     query_sum = jnp.dot(scaled, query_weight, preferred_element_type=jnp.float32)
     key_sum = jnp.dot(scaled, key_weight, preferred_element_type=jnp.float32)

time: 311 us -> 335 us (1.077)
  local copies, waits for them, and re-layouts: 19.5 us -> 35.6 us
  starting transfers between devices: 7.39 us -> 11.6 us
  waiting for transfers between devices: 228 us -> 232 us
    ppermute x0 -> x7, waiting for transfers between devices: none -> 77.9 us  [save_the_threads(): payload = jax.lax.ppermute(payload, 'tensor', kept_rows)]
    all_gather x1 -> x0, waiting for transfers between devices: 40.3 us -> none  [attend(): lax.all_gather(token_rows, 'tensor', axis=1, tiled=True).astype(jnp.float32)]
    all_to_all x1, waiting for transfers between devices: 32.7 us -> 0.01 us  [attend(): lax.all_to_all(spread, 'tensor', split_axis=3, concat_axis=1, tiled=True)]
    dynamic_update_slice x0 -> x8, local copies, waits for them, and re-layouts: none -> 14.3 us  [the longest x7 13.4 us: save_the_threads(): lax.dynamic_update_slice_in_dim(r_now, payload, (seen_now - no) % item_no...]
    ppermute x0 -> x7, starting transfers between devices: none -> 6.69 us  [save_the_threads(): payload = jax.lax.ppermute(payload, 'tensor', kept_rows)]
  transfers between devices with their start and end apart: 4 -> 10, of which waited for: 4 -> 9; matrix products, arithmetic and copies ran while one was open for 5% -> 9% of each run, Pallas kernels for 0% -> 0%
where the time goes in v1:
time: 335 us
  waiting for transfers between devices  232 us (69%)
  local copies, waits for them, and re-layouts  35.6 us (11%)
  matrix products  28.9 us (9%)
  between operations  13.8 us (4%)
  other arithmetic  12.2 us (4%)
  starting transfers between devices  11.6 us (3%)
    reduce_scatter x1, waiting for transfers between devices, attend(): lax.psum_scatter(partial_value, 'tensor', scatter_dimension=1, tiled=True)  147 us
    ppermute x7, waiting for transfers between devices, save_the_threads(): payload = jax.lax.ppermute(payload, 'tensor', kept_rows)  77.9 us
    dynamic_update_slice x7, local copies, waits for them, and re-layouts, save_the_threads(): lax.dynamic_update_slice_in_dim(r_now, payload, (seen_now - no) % item_no...  13.4 us
    dot_general x1, matrix products, attend(): jnp.dot(scaled, query_weight, preferred_element_type=jnp.float32)  9.67 us
    all_gather x1, waiting for transfers between devices, local(): everyone = lax.all_gather(mixed, 'worker', axis=0, tiled=True)  7.81 us
    dot_general x1, matrix products, attend(): jnp.dot(attended_rows, output_weight, preferred_element_type=jnp.float32)  6.79 us
  transfers between devices with their start and end apart: 10, of which 9 were waited for; matrix products, arithmetic and copies ran while one was open for 9% of the time, Pallas kernels for 0%

profile of v1, /device:TPU:0, one launch (start us, length us, event | category | flops | bytes accessed | tf_op | source)
XLA Modules:
  0.0 334.5 jit_solution(6947151480349560737)
XLA Ops:
  6.5 3.0 collective-permute-start
  9.5 2.5 copy.86
  12.1 1.3 copy.87
  13.4 4.9 %all-to-all-start = ((bf16[2,128,2,8,128]{4,1,0,2,3:T(8,128)(2,1)}), bf16[2,128,2,8,128]{4,1,0,2,3:T(8,128)(2,1)S(1)}, u32[]{:S(2)}, u32[]{:S(2)}) async-start(bf16[2,128,2,8,128]{4,1,0,2,3:T(8,128)(2,1)} %copy.87), calls=%async_computation | async-start | bytes 2097152 | tf_op jit(solution)/shard_map/all_to_all | solution.py:120
  18.3 8.2 %collective-permute-done = bf16[256,1024]{1,0:T(8,128)(2,1)} collective-permute-done((bf16[256,1024]{1,0:T(8,128)(2,1)}, bf16[256,1024]{1,0:T(8,128)(2,1)}, u32[]{:S(2)}, u32[]{:S(2)}) %collective-permute-start) | collective-permute-done | bytes 524320 | tf_op jit(solution)/shard_map/ppermute | solution.py:71
  26.5 3.7 %collective-permute-start.1 = (bf16[256,1024]{1,0:T(8,128)(2,1)}, bf16[256,1024]{1,0:T(8,128)(2,1)}, u32[]{:S(2)}, u32[]{:S(2)}) collective-permute-start(bf16[256,1024]{1,0:T(8,128)(2,1)} %collective-permute-done), channel_id=1, source_target_pairs={{0,1},{1,2},{2,3},{3,4},{4,5},{5,6},{6,7},{7,0},{8,9},{9,10},{10,1... | collective-permute-start | bytes 1572872 | tf_op jit(solution)/shard_map/ppermute | solution.py:71
  30.2 0.6 gather_fusion.2
  30.9 0.6 gather_fusion
  31.5 0.1 copy.80
  31.6 21.5 %collective-permute-done.1 = bf16[256,1024]{1,0:T(8,128)(2,1)} collective-permute-done((bf16[256,1024]{1,0:T(8,128)(2,1)}, bf16[256,1024]{1,0:T(8,128)(2,1)}, u32[]{:S(2)}, u32[]{:S(2)}) %collective-permute-start.1) | collective-permute-done | bytes 524320 | tf_op jit(solution)/shard_map/ppermute | solution.py:71
  53.2 4.0 %gather_fusion.1 = s32[1024,2]{1,0:T(8,128)} fusion(s32[2,64]{0,1:T(8,128)S(1)} %copy.80, s32[1024]{0:T(1024)S(1)} %broadcast_clamp_fusion), kind=kCustom, calls=%fused_computation.1 | custom fusion | bytes 20480 | tf_op jit(solution)/shard_map/jit(_take)/gather | solution.py:125
  57.2 1.2 copy.81
  58.4 10.8 %collective-permute-done.2 = bf16[256,1024]{1,0:T(8,128)(2,1)} collective-permute-done((bf16[256,1024]{1,0:T(8,128)(2,1)}, bf16[256,1024]{1,0:T(8,128)(2,1)}, u32[]{:S(2)}, u32[]{:S(2)}) %collective-permute-start.2) | collective-permute-done | bytes 524320 | tf_op jit(solution)/shard_map/ppermute | solution.py:71
  69.4 15.0 %collective-permute-done.3 = bf16[256,1024]{1,0:T(8,128)(2,1)S(1)} collective-permute-done((bf16[256,1024]{1,0:T(8,128)(2,1)}, bf16[256,1024]{1,0:T(8,128)(2,1)S(1)}, u32[]{:S(2)}, u32[]{:S(2)}) %collective-permute-start.3) | collective-permute-done | bytes 524320 | tf_op jit(solution)/shard_map/ppermute | solution.py:71
  84.4 0.5 multiply_cosine_fusion
  84.9 0.3 copy-done.5
  85.1 0.1 pad_maximum_fusion
  85.3 0.1 compare_bitcast_fusion
  85.4 13.1 %collective-permute-done.4 = bf16[256,1024]{1,0:T(8,128)(2,1)} collective-permute-done((bf16[256,1024]{1,0:T(8,128)(2,1)S(1)}, bf16[256,1024]{1,0:T(8,128)(2,1)}, u32[]{:S(2)}, u32[]{:S(2)}) %collective-permute-start.4) | collective-permute-done | bytes 524320 | tf_op jit(solution)/shard_map/ppermute | solution.py:71
  98.5 0.6 iota_compare_fusion
  99.1 2.4 broadcast_in_dim.106
  101.5 0.9 constant_dynamic-update-slice_fusion.7
  102.4 0.3 multiply_sine_fusion.1
  102.7 1.9 constant_dynamic-update-slice_fusion.6
  104.6 7.3 %collective-permute-done.5 = bf16[256,1024]{1,0:T(8,128)(2,1)} collective-permute-done((bf16[256,1024]{1,0:T(8,128)(2,1)}, bf16[256,1024]{1,0:T(8,128)(2,1)}, u32[]{:S(2)}, u32[]{:S(2)}) %collective-permute-start.5) | collective-permute-done | bytes 524320 | tf_op jit(solution)/shard_map/ppermute | solution.py:71
  111.9 1.9 constant_dynamic-update-slice_fusion.5
  113.8 1.9 constant_dynamic-update-slice_fusion.4
  115.7 1.1 copy.88
  116.8 1.9 constant_dynamic-update-slice_fusion.3
  118.8 1.9 constant_dynamic-update-slice_fusion.2
  120.7 1.9 constant_dynamic-update-slice_fusion.1
  122.6 2.0 collective-permute-done.6
  124.5 1.9 constant_dynamic-update-slice_fusion
  126.5 3.1 fusion.1
  129.6 3.6 %fusion.25 = bf16[256,128]{0,1:T(8,128)(2,1)S(1)} fusion(bf16[8192,128]{1,0:T(8,128)(2,1)S(1)} %copy-done, bf16[256,8192]{1,0:T(8,128)(2,1)} %constant_dynamic-update-slice_fusion, f32[8192]{0:T(1024)S(1)} %copy-done.10, f32[256]{0:T(256)S(1)} %add_rsqrt_fusion), kind=kOutput, calls=%fused_computation.28 | convolution fusion | flops 543227904 | bytes 6390784 | tf_op jit(solution)/shard_map/dot_general | solution.py:81
  133.2 0.6 reshape.302
  133.9 4.3 %fusion.31 = f32[256,128]{0,1:T(8,128)S(1)} fusion(bf16[8192,128]{1,0:T(8,128)(2,1)} %param.13, bf16[256,8192]{1,0:T(8,128)(2,1)} %constant_dynamic-update-slice_fusion, f32[8192]{0:T(1024)S(1)} %copy-done.10, f32[256]{0:T(256)S(1)} %add_rsqrt_fusion), kind=kOutput, calls=%fused_computation.30 | convolution fusion | flops 543260672 | bytes 6456320 | tf_op jit(solution)/shard_map/dot_general | solution.py:80
  138.2 0.1 copy.106
  138.4 9.7 %fusion.11 = f32[256,1024]{1,0:T(8,128)S(1)} fusion(bf16[8192,1024]{1,0:T(8,128)(2,1)} %param.12, bf16[256,8192]{1,0:T(8,128)(2,1)} %constant_dynamic-update-slice_fusion, f32[8192]{0:T(1024)S(1)} %copy-done.10, f32[256]{0:T(256)S(1)} %add_rsqrt_fusion), kind=kOutput, calls=%fused_computation.18 | convolution fusion | flops 4301520896 | bytes 22053888 | tf_op jit(solution)/shard_map/dot_general | solution.py:79
  148.0 0.3 copy.109
  148.4 0.9 slice_negate_fusion
  149.3 0.4 copy.104
  149.7 1.5 copy.105
  151.2 0.2 copy.110
  151.4 0.5 fusion.35
  151.9 0.3 fusion.69
  152.2 0.2 copy-done.3
  152.4 1.5 bitcast_reduce_fusion
  153.9 0.2 fusion.36
  154.1 2.1 fusion.3
  156.3 2.3 fusion.17
  158.6 0.4 fusion.18
  159.0 0.3 copy.96
  159.3 0.3 slice-done.2
  159.6 1.2 slice-done.3
  160.8 6.8 %fusion.38 = f32[256,8192]{1,0:T(8,128)} fusion(bf16[1024,8192]{1,0:T(8,128)(2,1)S(1)} %bitcast.101, bf16[32,8,8,128]{3,2,1,0:T(8,128)(2,1)S(1)} %bitcast.109), kind=kOutput, calls=%fused_computation.40 | convolution fusion | flops 4294967296 | bytes 25690112 | tf_op jit(solution)/shard_map/dot_general | solution.py:148
  167.7 146.7 %reduce-scatter.2.cloned.1.call-done = f32[256,1024]{1,0:T(8,128)} async-done(((f32[256,8192]{1,0:T(8,128)}), f32[256,1024]{1,0:T(8,128)}) %reduce-scatter.2.cloned.1.call-update) | async-done | bytes 1048592 | tf_op jit(solution)/shard_map/reduce_scatter | solution.py:149
  314.4 2.1 convert_element_type.67
  316.6 0.2 reduce-window.8
  316.8 0.1 select_reduce_fusion
  316.9 0.1 fusion.61
  317.0 7.8 %all-gather.2.cloned.1.call-done = bf16[512,1024]{1,0:T(8,128)(2,1)} async-done(((bf16[256,1024]{1,0:T(8,128)(2,1)}), bf16[512,1024]{1,0:T(8,128)(2,1)}) %all-gather.2.cloned.1.call-update) | async-done | bytes 1048592 | tf_op jit(solution)/shard_map/all_gather | solution.py:189
  324.8 1.8 gather_fusion.3
  326.7 1.0 fusion.37
  (58 shorter events, 0.5 us)
Async XLA Ops:
  6.5 123.0 %copy-start = (bf16[8192,128]{1,0:T(8,128)(2,1)S(1)}, bf16[8192,128]{1,0:T(8,128)(2,1)}, u32[]{:S(2)}) copy-start(bf16[8192,128]{1,0:T(8,128)(2,1)} %param.14) | copy-start | bytes 6291460
  6.5 23.7 %copy-start.2 = (s32[4]{0:T(128)S(1)}, s32[4]{0:T(128)}, u32[]{:S(2)}) copy-start(s32[4]{0:T(128)} %param.17) | copy-start | bytes 52
  6.5 24.3 %copy-start.8 = (s32[4,64]{1,0:T(4,128)S(1)}, s32[4,64]{1,0:T(4,128)}, u32[]{:S(2)}) copy-start(s32[4,64]{1,0:T(4,128)} %param.18) | copy-start | bytes 3076
  6.5 20.0 %collective-permute-start = (bf16[256,1024]{1,0:T(8,128)(2,1)}, bf16[256,1024]{1,0:T(8,128)(2,1)}, u32[]{:S(2)}, u32[]{:S(2)}) collective-permute-start(bf16[256,1024]{1,0:T(8,128)(2,1)} %param.10), channel_id=1, source_target_pairs={{0,1},{1,2},{2,3},{3,4},{4,5},{5,6},{6,7},{7,0},{8,9},{9,10},{10,1... | collective-permute-start | bytes 1572872 | tf_op jit(solution)/shard_map/ppermute | solution.py:71
  13.4 102.3 %all-to-all-start = ((bf16[2,128,2,8,128]{4,1,0,2,3:T(8,128)(2,1)}), bf16[2,128,2,8,128]{4,1,0,2,3:T(8,128)(2,1)S(1)}, u32[]{:S(2)}, u32[]{:S(2)}) async-start(bf16[2,128,2,8,128]{4,1,0,2,3:T(8,128)(2,1)} %copy.87), calls=%async_computation | async-start | bytes 2097152 | tf_op jit(solution)/shard_map/all_to_all | solution.py:120
  18.3 296.1 %reduce-scatter.2.cloned.1.call-start = ((), (), s32[]{:S(2)}) async-start(), calls=%async_computation.2 | async-start | bytes 9437184 | tf_op jit(solution)/shard_map/reduce_scatter | solution.py:149
  26.5 26.6 %collective-permute-start.1 = (bf16[256,1024]{1,0:T(8,128)(2,1)}, bf16[256,1024]{1,0:T(8,128)(2,1)}, u32[]{:S(2)}, u32[]{:S(2)}) collective-permute-start(bf16[256,1024]{1,0:T(8,128)(2,1)} %collective-permute-done), channel_id=1, source_target_pairs={{0,1},{1,2},{2,3},{3,4},{4,5},{5,6},{6,7},{7,0},{8,9},{9,10},{10,1... | collective-permute-start | bytes 1572872 | tf_op jit(solution)/shard_map/ppermute | solution.py:71
  53.1 16.1 %collective-permute-start.2 = (bf16[256,1024]{1,0:T(8,128)(2,1)}, bf16[256,1024]{1,0:T(8,128)(2,1)}, u32[]{:S(2)}, u32[]{:S(2)}) collective-permute-start(bf16[256,1024]{1,0:T(8,128)(2,1)} %collective-permute-done.1), channel_id=1, source_target_pairs={{0,1},{1,2},{2,3},{3,4},{4,5},{5,6},{6,7},{7,0},{8,9},{9,10},{10,1... | collective-permute-start | bytes 1572872 | tf_op jit(solution)/shard_map/ppermute | solution.py:71
  69.3 15.1 %collective-permute-start.3 = (bf16[256,1024]{1,0:T(8,128)(2,1)}, bf16[256,1024]{1,0:T(8,128)(2,1)S(1)}, u32[]{:S(2)}, u32[]{:S(2)}) collective-permute-start(bf16[256,1024]{1,0:T(8,128)(2,1)} %collective-permute-done.2), channel_id=1, source_target_pairs={{0,1},{1,2},{2,3},{3,4},{4,5},{5,6},{6,7},{7,0},{8,9},{9,10},{10,1... | collective-permute-start | bytes 1572872 | tf_op jit(solution)/shard_map/ppermute | solution.py:71
  84.3 0.8 copy-start.5
  84.4 14.1 %collective-permute-start.4 = (bf16[256,1024]{1,0:T(8,128)(2,1)S(1)}, bf16[256,1024]{1,0:T(8,128)(2,1)}, u32[]{:S(2)}, u32[]{:S(2)}) collective-permute-start(bf16[256,1024]{1,0:T(8,128)(2,1)S(1)} %collective-permute-done.3), channel_id=1, source_target_pairs={{0,1},{1,2},{2,3},{3,4},{4,5},{5,6},{6,7},{7,0},{8,9},{9,10},{10,1... | collective-permute-start | bytes 1572872 | tf_op jit(solution)/shard_map/ppermute | solution.py:71
  98.5 13.5 %collective-permute-start.5 = (bf16[256,1024]{1,0:T(8,128)(2,1)}, bf16[256,1024]{1,0:T(8,128)(2,1)}, u32[]{:S(2)}, u32[]{:S(2)}) collective-permute-start(bf16[256,1024]{1,0:T(8,128)(2,1)} %collective-permute-done.4), channel_id=1, source_target_pairs={{0,1},{1,2},{2,3},{3,4},{4,5},{5,6},{6,7},{7,0},{8,9},{9,10},{10,1... | collective-permute-start | bytes 1572872 | tf_op jit(solution)/shard_map/ppermute | solution.py:71
  99.1 2.4 copy-start.4
  111.9 12.6 %collective-permute-start.6 = (bf16[256,1024]{1,0:T(8,128)(2,1)}, bf16[256,1024]{1,0:T(8,128)(2,1)}, u32[]{:S(2)}, u32[]{:S(2)}) collective-permute-start(bf16[256,1024]{1,0:T(8,128)(2,1)} %collective-permute-done.5), channel_id=1, source_target_pairs={{0,1},{1,2},{2,3},{3,4},{4,5},{5,6},{6,7},{7,0},{8,9},{9,10},{10,1... | collective-permute-start | bytes 1572872 | tf_op jit(solution)/shard_map/ppermute | solution.py:71
  116.8 12.7 %copy-start.10 = (f32[8192]{0:T(1024)S(1)}, f32[8192]{0:T(1024)}, u32[]{:S(2)}) copy-start(f32[8192]{0:T(1024)} %param.11) | copy-start | bytes 98308
  149.7 2.2 copy-start.6
  151.2 1.2 copy-start.3
  154.1 5.2 %slice-start = ((s8[16777216]{0:T(1024)(128)(4,1)}), s8[4194304]{0:T(1024)(128)(4,1)S(1)}, s32[]{:S(2)}) async-start(s8[16777216]{0:T(1024)(128)(4,1)} %bitcast.100), calls=%async_computation.4 | async-start | bytes 8388608
  156.2 2.3 copy-start.7
  156.2 3.1 slice-start.1
  156.2 3.4 %slice-start.2 = ((s8[16777216]{0:T(1024)(128)(4,1)}), s8[4194304]{0:T(1024)(128)(4,1)S(1)}, s32[]{:S(2)}) async-start(s8[16777216]{0:T(1024)(128)(4,1)} %bitcast.100), calls=%async_computation.6 | async-start | bytes 8388608
  156.3 4.6 %slice-start.3 = ((s8[16777216]{0:T(1024)(128)(4,1)}), s8[4194304]{0:T(1024)(128)(4,1)S(1)}, s32[]{:S(2)}) async-start(s8[16777216]{0:T(1024)(128)(4,1)} %bitcast.100), calls=%async_computation.7 | async-start | bytes 8388608
  167.6 148.9 %copy-start.9 = (s32[4]{0:T(128)S(1)}, s32[4]{0:T(128)}, u32[]{:S(2)}) copy-start(s32[4]{0:T(128)} %param.19) | copy-start | bytes 52
  167.6 160.1 %copy-start.1 = (bf16[8192,128]{1,0:T(8,128)(2,1)S(1)}, bf16[8192,128]{1,0:T(8,128)(2,1)}, u32[]{:S(2)}) copy-start(bf16[8192,128]{1,0:T(8,128)(2,1)} %param.14) | copy-start | bytes 6291460
  167.7 157.2 %all-gather.2.cloned.1.call-start = ((), (), s32[]{:S(2)}) async-start(), calls=%async_computation.3 | async-start | bytes 1572864 | tf_op jit(solution)/shard_map/all_gather | solution.py:189
Sparse Core Ops, SparseCore 0:
  167.8 146.6 reduce-scatter.1
  316.7 8.1 all-gather.1
